TPU v7x, 32 devices: a whole 2x2x4 slice. The times are simulated.
32 devices in a mesh: wide: 8 (over y, x, core), narrow: 4 (over z).
Axes of the slice: x: 2, y: 2, z: 4, core: 2. Of those that a mesh axis runs over, the one named last changes fastest.
Arguments:
- tokens: bfloat16 [4096, 1024], P(('wide', 'narrow')), may hold values from -6 to 6
- log_decay: float32 [8, 4096], P(None, 'wide'), as said below
- lengths: int32 [1], replicated, may hold values from 1024 to 4096, as said below
- pad_counts: int32 [1], replicated, may hold values from 0 to 255
- w_query: bfloat16 [1024, 1024], replicated, may hold values from -0.1875 to 0.1875
- w_key: bfloat16 [1024, 1024], replicated, may hold values from -0.1875 to 0.1875
- w_value: bfloat16 [1024, 1024], replicated, may hold values from -0.1875 to 0.1875
- w_gate: bfloat16 [1024, 1024], replicated, may hold values from -0.1875 to 0.1875
- w_out: bfloat16 [1024, 1024], replicated, may hold values from -0.375 to 0.375
- w_first: bfloat16 [1024, 2816], P(None, 'narrow'), may hold values from -0.1875 to 0.1875
- w_second: bfloat16 [1024, 2816], P(None, 'narrow'), may hold values from -0.1875 to 0.1875
- w_third: bfloat16 [2816, 1024], P('narrow'), may hold values from -0.109375 to 0.109375
- cotangent: bfloat16 [4096, 1024], P(('wide', 'narrow')), may hold values from -6 to 6
Outputs:
- output: bfloat16 [4096, 1024], P(('wide', 'narrow'))
- grad_tokens: float32 [4096, 1024], P(('wide', 'narrow'))
- grad_w_query: float32 [1024, 1024], replicated
- grad_w_key: float32 [1024, 1024], replicated
- grad_w_value: float32 [1024, 1024], replicated
- grad_w_gate: float32 [1024, 1024], replicated
- grad_w_out: float32 [1024, 1024], replicated
- grad_w_first: float32 [1024, 2816], P(None, 'narrow')
- grad_w_second: float32 [1024, 2816], P(None, 'narrow')
- grad_w_third: float32 [2816, 1024], P('narrow')
Inputs may be any that keep to these rules, and one draw needn't show every extreme that they name: `lengths`: multiples of 256 that sum to 4096; the longest is exactly 4096. `log_decay`: strictly negative.
All inputs are finite; a program needn't handle non-finite values.
Results may differ from a plain program's by a relative error of at most 0.017.
Values may be sent and summed in bfloat16 or wider, within the bound.
No kernel may reach another device: no remote copies, remote signals or barrier semaphores. Data moves between devices by JAX's collectives and lax.ppermute only.
A program may use at most 192 MiB of HBM per device.

v0:
```python
import jax
import jax.numpy as jnp
from jax import lax
from jax.sharding import PartitionSpec as P

BLOCK = 256
LONGEST = 8192
epsilon = 1e-06
precise = lax.Precision.HIGHEST


def from_behind(block, axis, distance):
    devices = range(lax.axis_size(axis))
    route = [(i - distance, i) for i in devices if i - distance in devices]
    return lax.ppermute(block, axis, route)


def rms_norm(values):
    return values * lax.rsqrt(jnp.mean(values * values, axis=-1, keepdims=True) + epsilon)


def rms_back(values, gradient):
    inverse_rms = lax.rsqrt(jnp.mean(values * values, axis=-1, keepdims=True) + epsilon)
    normed = values * inverse_rms
    return inverse_rms * (gradient - normed * jnp.mean(gradient * normed, axis=-1, keepdims=True))


def silu_slope(values):
    squashed = jax.nn.sigmoid(values)
    return squashed * (1.0 + values * (1.0 - squashed))


def token_layout(lengths, pad_counts, anchor, total_rows):
    ends = jnp.cumsum(lengths, dtype=jnp.int32)
    starts = ends - lengths
    position = anchor + jnp.arange(total_rows, dtype=jnp.int32)
    inside = (position[:, None] >= starts[None, :]) & (position[:, None] < ends[None, :])
    limit = jnp.sum(jnp.where(inside, (ends - pad_counts)[None, :], 0), axis=1, dtype=jnp.int32)
    live = (position < limit).astype(jnp.float32)
    opening = jnp.any(position[:, None] == starts[None, :], axis=1).astype(jnp.float32)
    return (live, opening)


def project(left_hand, right_hand):
    return jnp.dot(left_hand, right_hand, preferred_element_type=jnp.float32)


def weight_grad(left_hand, right_hand):
    return jnp.einsum("tc,td->cd", left_hand, right_hand, preferred_element_type=jnp.float32)


def transposed(left_hand, right_hand):
    return jnp.einsum("td,cd->tc", left_hand, right_hand, preferred_element_type=jnp.float32)


def to_blocks(values, head_count, block_len):
    row_count, model_width = values.shape
    shaped = values.reshape(
        row_count // block_len, block_len, head_count, model_width // head_count
    )
    return shaped.transpose(0, 2, 1, 3)


def from_blocks(values):
    block_count, head_count, block_len, head_size = values.shape
    return values.transpose(0, 2, 1, 3).reshape(block_count * block_len, head_count * head_size)


def body(
    tokens,
    log_decay,
    lengths,
    pad_counts,
    w_query,
    w_key,
    w_value,
    w_gate,
    w_out,
    w_first,
    w_second,
    w_third,
    cotangent,
):
    head_count = log_decay.shape[0]
    local_rows = log_decay.shape[1]
    share_rows = tokens.shape[0]
    block_len = BLOCK
    block_count = local_rows // block_len
    own_start = lax.axis_index("narrow") * share_rows
    live, opening = token_layout(
        lengths, pad_counts, lax.axis_index("wide") * local_rows, local_rows
    )
    keep_block = 1.0 - opening.reshape(block_count, block_len)[:, 0]
    whole_rows = lax.all_gather(tokens, "narrow", axis=0, tiled=True)
    normed_one = rms_norm(whole_rows.astype(jnp.float32)).astype(jnp.bfloat16)
    query_lin = project(normed_one, w_query)
    key_lin = project(normed_one, w_key)
    value_lin = project(normed_one, w_value)
    gate_act = jax.nn.sigmoid(project(normed_one, w_gate))
    query_blk = to_blocks(jax.nn.silu(query_lin).astype(jnp.bfloat16), head_count, block_len)
    key_blk = to_blocks(
        (jax.nn.silu(key_lin) * live[:, None]).astype(jnp.bfloat16), head_count, block_len
    )
    value_blk = to_blocks(value_lin.astype(jnp.bfloat16), head_count, block_len)
    cumulative = jnp.cumsum(
        log_decay.reshape(head_count, block_count, block_len), axis=2
    ).transpose(1, 0, 2)
    positions = jnp.arange(block_len, dtype=jnp.int32)
    causal = positions[:, None] >= positions[None, :]
    spread = cumulative[:, :, :, None] - cumulative[:, :, None, :]
    weights = jnp.where(causal, jnp.exp(jnp.where(causal, spread, 0.0)), 0.0)
    rise = jnp.exp(cumulative)
    tail = jnp.exp(cumulative[:, :, -1:] - cumulative)
    block_decay = jnp.exp(cumulative[:, :, -1]) * keep_block[:, None]
    query_float = query_blk.astype(jnp.float32)
    key_tail = key_blk.astype(jnp.float32) * tail[..., None]
    value_float = value_blk.astype(jnp.float32)
    contrib = jnp.einsum("bhsd,bhse->bhde", key_tail, value_float, precision=precise)

    def run_states(carry, inputs):
        decay_now, contrib_now = inputs
        return (decay_now[:, None, None] * carry + contrib_now, carry)

    zero_state = jnp.zeros(contrib.shape[1:], jnp.float32)
    local_final, local_enter = lax.scan(run_states, zero_state, (block_decay, contrib))
    factor_all = jnp.prod(block_decay, axis=0)
    ones_row = jnp.ones((1, head_count), jnp.float32)
    prefix = jnp.cumprod(jnp.concatenate([ones_row, block_decay[:-1]], axis=0), axis=0)
    after_factor = jnp.flip(
        jnp.cumprod(jnp.flip(jnp.concatenate([block_decay[1:], ones_row], axis=0), 0), axis=0), 0
    )
    hop_count = min(lax.axis_size("wide") - 1, LONGEST // local_rows + 1)

    def relay_step(step_index, incoming):
        return from_behind(factor_all[:, None, None] * incoming + local_final, "wide", 1)

    incoming = lax.fori_loop(0, hop_count, relay_step, zero_state)
    entering = local_enter + prefix[:, :, None, None] * incoming[None]
    kept_enter = entering * keep_block[:, None, None, None]
    raw_scores = jnp.einsum(
        "bhtd,bhsd->bhts", query_blk, key_blk, preferred_element_type=jnp.float32
    )
    scores = (raw_scores * weights).astype(jnp.bfloat16)
    intra = jnp.einsum("bhts,bhsd->bhtd", scores, value_blk, preferred_element_type=jnp.float32)
    query_rise = query_float * rise[..., None]
    inter = jnp.einsum("bhtd,bhde->bhte", query_rise, kept_enter, precision=precise)
    attended = from_blocks(intra + inter)
    attn_normed = rms_norm(attended)
    gated = (attn_normed * gate_act).astype(jnp.bfloat16)
    gated_own = lax.dynamic_slice_in_dim(gated, own_start, share_rows, 0)
    hidden_state = tokens.astype(jnp.float32) + project(gated_own, w_out)
    normed_two = rms_norm(hidden_state).astype(jnp.bfloat16)
    gathered_two = lax.all_gather(normed_two, "narrow", axis=0, tiled=True)
    first_lin = project(gathered_two, w_first)
    second_lin = project(gathered_two, w_second)
    product = (first_lin * second_lin).astype(jnp.bfloat16)
    ffn_own = lax.psum_scatter(
        project(product, w_third).astype(jnp.bfloat16), "narrow", scatter_dimension=0, tiled=True
    ).astype(jnp.float32)
    output = (hidden_state + ffn_own).astype(jnp.bfloat16)
    grad_whole = lax.all_gather(cotangent, "narrow", axis=0, tiled=True)
    grad_w_third = weight_grad(product, grad_whole)
    grad_product = transposed(grad_whole, w_third)
    grad_first = (grad_product * second_lin).astype(jnp.bfloat16)
    grad_second = (grad_product * first_lin).astype(jnp.bfloat16)
    grad_w_first = weight_grad(gathered_two, grad_first)
    grad_w_second = weight_grad(gathered_two, grad_second)
    grad_normed_two = lax.psum_scatter(
        transposed(grad_first, w_first) + transposed(grad_second, w_second),
        "narrow",
        scatter_dimension=0,
        tiled=True,
    )
    grad_hidden = cotangent.astype(jnp.float32) + rms_back(hidden_state, grad_normed_two)
    grad_hidden_low = grad_hidden.astype(jnp.bfloat16)
    grad_hidden_whole = lax.all_gather(grad_hidden_low, "narrow", axis=0, tiled=True)
    grad_gated = transposed(grad_hidden_whole, w_out)
    grad_gate_lin = (grad_gated * attn_normed * gate_act * (1.0 - gate_act)).astype(jnp.bfloat16)
    grad_attended = rms_back(attended, grad_gated * gate_act).astype(jnp.bfloat16)
    grad_blk = to_blocks(grad_attended, head_count, block_len)
    grad_float = grad_blk.astype(jnp.float32)
    grad_value = jnp.einsum("bhts,bhtd->bhsd", scores, grad_blk, preferred_element_type=jnp.float32)
    grad_raw = (
        jnp.einsum("bhtd,bhsd->bhts", grad_blk, value_blk, preferred_element_type=jnp.float32)
        * weights
    ).astype(jnp.bfloat16)
    grad_query = jnp.einsum(
        "bhts,bhsd->bhtd", grad_raw, key_blk, preferred_element_type=jnp.float32
    )
    grad_key = jnp.einsum(
        "bhts,bhtd->bhsd", grad_raw, query_blk, preferred_element_type=jnp.float32
    )
    grad_query = grad_query + rise[..., None] * jnp.einsum(
        "bhte,bhde->bhtd", grad_float, kept_enter, precision=precise
    )
    enter_direct = keep_block[:, None, None, None] * jnp.einsum(
        "bhtd,bhte->bhde", query_rise, grad_float, precision=precise
    )

    def back_states(carry, inputs):
        decay_now, direct_now = inputs
        return (direct_now + decay_now[:, None, None] * carry, carry)

    local_first, local_after = lax.scan(
        back_states, zero_state, (block_decay, enter_direct), reverse=True
    )
    hop_count = min(lax.axis_size("wide") - 1, LONGEST // local_rows + 1)

    def relay_back(step_index, arriving):
        return from_behind(
            (factor_all[:, None, None] * arriving + local_first).astype(jnp.bfloat16), "wide", -1
        ).astype(jnp.float32)

    arriving = lax.fori_loop(0, hop_count, relay_back, zero_state)
    grad_contrib = local_after + after_factor[:, :, None, None] * arriving[None]
    grad_key = grad_key + tail[..., None] * jnp.einsum(
        "bhse,bhde->bhsd", value_float, grad_contrib, precision=precise
    )
    grad_value = grad_value + jnp.einsum(
        "bhsd,bhde->bhse", key_tail, grad_contrib, precision=precise
    )
    grad_query_lin = (from_blocks(grad_query) * silu_slope(query_lin)).astype(jnp.bfloat16)
    grad_key_lin = (from_blocks(grad_key) * live[:, None] * silu_slope(key_lin)).astype(
        jnp.bfloat16
    )
    grad_value_lin = from_blocks(grad_value).astype(jnp.bfloat16)
    grad_normed_one = (
        transposed(grad_query_lin, w_query)
        + transposed(grad_key_lin, w_key)
        + transposed(grad_value_lin, w_value)
        + transposed(grad_gate_lin, w_gate)
    )
    grad_own = lax.dynamic_slice_in_dim(grad_normed_one, own_start, share_rows, 0)
    grad_tokens = grad_hidden + rms_back(tokens.astype(jnp.float32), grad_own)
    summed = (
        lax.psum(weight_grad(normed_one, grad_query_lin).astype(jnp.bfloat16), "wide").astype(
            jnp.float32
        ),
        lax.psum(weight_grad(normed_one, grad_key_lin).astype(jnp.bfloat16), "wide").astype(
            jnp.float32
        ),
        lax.psum(weight_grad(normed_one, grad_value_lin).astype(jnp.bfloat16), "wide").astype(
            jnp.float32
        ),
        lax.psum(weight_grad(normed_one, grad_gate_lin).astype(jnp.bfloat16), "wide").astype(
            jnp.float32
        ),
        lax.psum(weight_grad(gated, grad_hidden_whole).astype(jnp.bfloat16), "wide").astype(
            jnp.float32
        ),
        lax.psum(grad_w_first.astype(jnp.bfloat16), "wide").astype(jnp.float32),
        lax.psum(grad_w_second.astype(jnp.bfloat16), "wide").astype(jnp.float32),
        lax.psum(grad_w_third.astype(jnp.bfloat16), "wide").astype(jnp.float32),
    )
    mixer_total = summed[:5]
    glu_total = summed[5:]
    return (
        output,
        grad_tokens,
        mixer_total[0],
        mixer_total[1],
        mixer_total[2],
        mixer_total[3],
        mixer_total[4],
        glu_total[0],
        glu_total[1],
        glu_total[2],
    )


def solution(mesh):
    in_specs = (
        P(("wide", "narrow"), None),
        P(None, "wide"),
        P(),
        P(),
        P(),
        P(),
        P(),
        P(),
        P(),
        P(None, "narrow"),
        P(None, "narrow"),
        P("narrow", None),
        P(("wide", "narrow"), None),
    )
    out_specs = (
        P(("wide", "narrow"), None),
        P(("wide", "narrow"), None),
        P(),
        P(),
        P(),
        P(),
        P(),
        P(None, "narrow"),
        P(None, "narrow"),
        P("narrow", None),
    )
    return jax.shard_map(body, mesh=mesh, in_specs=in_specs, out_specs=out_specs, check_vma=False)
```

profile of v0, /device:TPU:0, one launch (start us, length us, event | category | flops | bytes accessed | tf_op | source)
XLA Modules:
  0.0 669.6 jit_solution(619893740103989016)
XLA Ops:
  12.5 27.8 %all-gather.5.cloned.1.call-done = bf16[512,1024]{1,0:T(8,128)(2,1)} async-done(((bf16[128,1024]{1,0:T(8,128)(2,1)}), bf16[512,1024]{1,0:T(8,128)(2,1)}) %all-gather.5.cloned.1.call-update) | async-done | bytes 1048592 | tf_op jit(solution)/shard_map/all_gather | solution.py:94
  41.8 3.2 fusion.96
  48.4 2.4 copy.127
  50.8 3.2 fusion.94
  59.9 3.5 fusion.12
  64.6 4.0 while.52
  68.6 2.4 copy.107
  71.0 3.1 multiply_convert_fusion.1
  76.3 73.5 %while.51 = (s32[]{:T(128)}, f32[8,128,128]{2,1,0:T(8,128)S(1)}, f32[8]{0:T(128)S(1)}, f32[8,128,128]{2,1,0:T(8,128)S(1)}, s32[]{:T(128)}) while((s32[]{:T(128)}, f32[8,128,128]{2,1,0:T(8,128)S(1)}, f32[8]{0:T(128)S(1)}, f32[8,128,128]{2,1,0:T(8,128)S(1)}, s32[]{:T(128)}) %tuple.105), condition=%wide.region_8.9_spmd, body=%wide.region_7.8_spmd.sunk | while | flops 262146 | bytes 3670149 | solution.py:137
  81.2 8.8 %collective-permute-start = (f32[8,128,128]{2,1,0:T(8,128)}, f32[8,128,128]{2,1,0:T(8,128)S(1)}, u32[]{:S(2)}, u32[]{:S(2)}) collective-permute-start(f32[8,128,128]{2,1,0:T(8,128)} %multiply_add_fusion.6), channel_id=1, source_target_pairs={{0,4},{4,8},{8,12},{12,16},{16,20},{20,24},{24,28},{1,5},{5,9},{9,... | collective-permute-start | bytes 1572872 | tf_op jit(solution)/shard_map/while/body/eval_jaxpr/ppermute | solution.py:15
  92.6 9.0 %collective-permute-start = (f32[8,128,128]{2,1,0:T(8,128)}, f32[8,128,128]{2,1,0:T(8,128)S(1)}, u32[]{:S(2)}, u32[]{:S(2)}) collective-permute-start(f32[8,128,128]{2,1,0:T(8,128)} %multiply_add_fusion.6), channel_id=1, source_target_pairs={{0,4},{4,8},{8,12},{12,16},{16,20},{20,24},{24,28},{1,5},{5,9},{9,... | collective-permute-start | bytes 1572872 | tf_op jit(solution)/shard_map/while/body/eval_jaxpr/ppermute | solution.py:15
  104.2 9.0 %collective-permute-start = (f32[8,128,128]{2,1,0:T(8,128)}, f32[8,128,128]{2,1,0:T(8,128)S(1)}, u32[]{:S(2)}, u32[]{:S(2)}) collective-permute-start(f32[8,128,128]{2,1,0:T(8,128)} %multiply_add_fusion.6), channel_id=1, source_target_pairs={{0,4},{4,8},{8,12},{12,16},{16,20},{20,24},{24,28},{1,5},{5,9},{9,... | collective-permute-start | bytes 1572872 | tf_op jit(solution)/shard_map/while/body/eval_jaxpr/ppermute | solution.py:15
  115.8 9.0 %collective-permute-start = (f32[8,128,128]{2,1,0:T(8,128)}, f32[8,128,128]{2,1,0:T(8,128)S(1)}, u32[]{:S(2)}, u32[]{:S(2)}) collective-permute-start(f32[8,128,128]{2,1,0:T(8,128)} %multiply_add_fusion.6), channel_id=1, source_target_pairs={{0,4},{4,8},{8,12},{12,16},{16,20},{20,24},{24,28},{1,5},{5,9},{9,... | collective-permute-start | bytes 1572872 | tf_op jit(solution)/shard_map/while/body/eval_jaxpr/ppermute | solution.py:15
  127.4 9.0 %collective-permute-start = (f32[8,128,128]{2,1,0:T(8,128)}, f32[8,128,128]{2,1,0:T(8,128)S(1)}, u32[]{:S(2)}, u32[]{:S(2)}) collective-permute-start(f32[8,128,128]{2,1,0:T(8,128)} %multiply_add_fusion.6), channel_id=1, source_target_pairs={{0,4},{4,8},{8,12},{12,16},{16,20},{20,24},{24,28},{1,5},{5,9},{9,... | collective-permute-start | bytes 1572872 | tf_op jit(solution)/shard_map/while/body/eval_jaxpr/ppermute | solution.py:15
  139.0 9.0 %collective-permute-start = (f32[8,128,128]{2,1,0:T(8,128)}, f32[8,128,128]{2,1,0:T(8,128)S(1)}, u32[]{:S(2)}, u32[]{:S(2)}) collective-permute-start(f32[8,128,128]{2,1,0:T(8,128)} %multiply_add_fusion.6), channel_id=1, source_target_pairs={{0,4},{4,8},{8,12},{12,16},{16,20},{20,24},{24,28},{1,5},{5,9},{9,... | collective-permute-start | bytes 1572872 | tf_op jit(solution)/shard_map/while/body/eval_jaxpr/ppermute | solution.py:15
  149.9 6.0 multiply_reduce_fusion.1
  155.9 2.9 copy.119
  158.9 5.0 multiply_convert_fusion.4
  166.6 40.0 %all-gather.7.cloned.1.call-done = bf16[512,1024]{1,0:T(8,128)(2,1)} async-done(((bf16[128,1024]{1,0:T(8,128)(2,1)}), bf16[512,1024]{1,0:T(8,128)(2,1)}) %all-gather.7.cloned.1.call-update) | async-done | bytes 1048592 | tf_op jit(solution)/shard_map/all_gather | solution.py:153
  206.6 3.9 fusion.100
  212.5 23.0 %all-gather.9.cloned.1.call-done = bf16[512,1024]{1,0:T(8,128)(2,1)} async-done(((bf16[128,1024]{1,0:T(8,128)(2,1)}), bf16[512,1024]{1,0:T(8,128)(2,1)}) %all-gather.9.cloned.1.call-update) | async-done | bytes 1048592 | tf_op jit(solution)/shard_map/all_gather | solution.py:161
  235.5 4.5 multiply_convert_fusion.7
  244.4 43.1 %reduce-scatter.5.cloned.1.call-done = f32[128,1024]{1,0:T(8,128)} async-done(((f32[512,1024]{1,0:T(8,128)}), f32[128,1024]{1,0:T(8,128)}) %reduce-scatter.5.cloned.1.call-update) | async-done | bytes 524304 | tf_op jit(solution)/shard_map/reduce_scatter | solution.py:168
  292.1 3.6 convolution_convert_fusion.8
  296.0 3.7 convolution_convert_fusion.6
  303.8 14.3 %all-gather.11.cloned.1.call-done = bf16[512,1024]{1,0:T(8,128)(2,1)} async-done(((bf16[128,1024]{1,0:T(8,128)(2,1)}), bf16[512,1024]{1,0:T(8,128)(2,1)}) %all-gather.11.cloned.1.call-update) | async-done | bytes 1048592 | tf_op jit(solution)/shard_map/all_gather | solution.py:176
  318.1 6.1 multiply_reduce_fusion
  335.2 4.0 while.53
  339.2 67.9 %while.54 = (s32[]{:T(128)}, f32[8,128,128]{2,1,0:T(8,128)}, f32[8]{0:T(128)S(1)}, f32[8,128,128]{2,1,0:T(8,128)S(1)}, s32[]{:T(128)}, /*index=5*/s32[]{:T(128)}) while((s32[]{:T(128)}, f32[8,128,128]{2,1,0:T(8,128)}, f32[8]{0:T(128)S(1)}, f32[8,128,128]{2,1,0:T(8,128)S(1)}, s32[]{:T(128)}, /*index=5*/s32[]{:T(128)}) %tuple.129), condition=%wide.region_20.21_spmd.clone, body=%wide.region_19.20_spmd.clone.sunk | while | flops 655363 | bytes 3145879 | solution.py:214
  347.7 5.6 collective-permute-done.1
  357.4 6.6 collective-permute-done.1
  368.0 6.6 collective-permute-done.1
  378.5 6.6 collective-permute-done.1
  389.1 6.6 collective-permute-done.1
  399.7 6.6 collective-permute-done.1
  407.2 4.1 fusion.11
  422.3 2.6 convolution_convert_fusion
  425.0 2.7 convolution_convert_fusion.4
  428.6 2.7 convolution_convert_fusion.3
  431.3 2.7 convolution_convert_fusion.2
  434.0 2.7 convolution_convert_fusion.1
  437.8 2.8 fusion.106
  449.5 193.0 %all-reduce.4.cloned.1.call-done = (bf16[1024,1024]{1,0:T(8,128)(2,1)}, bf16[1024,1024]{1,0:T(8,128)(2,1)}, bf16[1024,1024]{1,0:T(8,128)(2,1)}, bf16[1024,1024]{...) async-done(((bf16[1024,1024]{1,0:T(8,128)(2,1)}, ...) | async-done | bytes 14811152 | tf_op jit(solution)/shard_map/psum | solution.py:236
  642.5 4.2 convert_element_type.176
  646.8 2.5 convert_element_type.178
  649.2 2.5 convert_element_type.180
  651.7 2.5 convert_element_type.182
  654.2 2.5 convert_element_type.184
  (317 shorter events, 131.1 us)
Async XLA Ops:
  7.2 151.7 %copy-start = (bf16[1024,1024]{1,0:T(8,128)(2,1)S(1)}, bf16[1024,1024]{1,0:T(8,128)(2,1)}, u32[]{:S(2)}) copy-start(bf16[1024,1024]{1,0:T(8,128)(2,1)} %param.28) | copy-start | bytes 6291460
  7.2 33.1 %all-gather.5.cloned.1.call-start = ((), (), s32[]{:S(2)}) async-start(), calls=%async_computation.2 | async-start | bytes 1310720 | tf_op jit(solution)/shard_map/all_gather | solution.py:94
  7.9 198.6 %all-gather.7.cloned.1.call-start = ((), (), s32[]{:S(2)}) async-start(), calls=%async_computation.3 | async-start | bytes 1310720 | tf_op jit(solution)/shard_map/all_gather | solution.py:153
  10.1 35.0 %copy-start.59 = (f32[8,2,2]{0,1,2:T(2,128)}, f32[8,2,2]{0,1,2:T(2,128)S(1)}, u32[]{:S(2)}) copy-start(f32[8,2,2]{0,1,2:T(2,128)S(1)} %copy.112) | copy-start | bytes 388
  11.5 138.4 %copy-start.70 = (f32[2]{0:T(128)}, f32[2]{0:T(128)S(1)}, u32[]{:S(2)}) copy-start(f32[2]{0:T(128)S(1)} %fusion.84) | copy-start | bytes 28
  11.6 59.4 %copy-start.57 = (f32[2,8,256]{2,1,0:T(8,128)}, f32[2,8,256]{2,1,0:T(8,128)S(1)}, u32[]{:S(2)}) copy-start(f32[2,8,256]{2,1,0:T(8,128)S(1)} %bitcast_bitcast_fusion.1) | copy-start | bytes 49156
  11.7 33.3 %copy-start.64 = (f32[2,8]{1,0:T(2,128)}, f32[2,8]{1,0:T(2,128)S(1)}, u32[]{:S(2)}) copy-start(f32[2,8]{1,0:T(2,128)S(1)} %slice_reduce_fusion) | copy-start | bytes 196
  12.4 137.5 %copy-start.65 = (f32[2,8]{1,0:T(2,128)}, f32[2,8]{1,0:T(2,128)S(1)}, u32[]{:S(2)}) copy-start(f32[2,8]{1,0:T(2,128)S(1)} %reduce_window.14) | copy-start | bytes 196
  12.4 41.6 %copy-start.62 = (f32[512]{0:T(512)}, f32[512]{0:T(512)S(1)}, u32[]{:S(2)}) copy-start(f32[512]{0:T(512)S(1)} %fusion.81) | copy-start | bytes 6148
  41.8 117.0 %copy-start.74 = (f32[512]{0:T(512)}, f32[512]{0:T(512)S(1)}, u32[]{:S(2)}) copy-start(f32[512]{0:T(512)S(1)} %add_rsqrt_fusion) | copy-start | bytes 6148
  58.8 4.6 copy-start.10
  68.6 5.5 copy-start.72
  77.2 3.0 collective-permute-start
  81.2 10.5 %collective-permute-start = (f32[8,128,128]{2,1,0:T(8,128)}, f32[8,128,128]{2,1,0:T(8,128)S(1)}, u32[]{:S(2)}, u32[]{:S(2)}) collective-permute-start(f32[8,128,128]{2,1,0:T(8,128)} %multiply_add_fusion.6), channel_id=1, source_target_pairs={{0,4},{4,8},{8,12},{12,16},{16,20},{20,24},{24,28},{1,5},{5,9},{9,... | collective-permute-start | bytes 1572872 | tf_op jit(solution)/shard_map/while/body/eval_jaxpr/ppermute | solution.py:15
  92.6 10.7 %collective-permute-start = (f32[8,128,128]{2,1,0:T(8,128)}, f32[8,128,128]{2,1,0:T(8,128)S(1)}, u32[]{:S(2)}, u32[]{:S(2)}) collective-permute-start(f32[8,128,128]{2,1,0:T(8,128)} %multiply_add_fusion.6), channel_id=1, source_target_pairs={{0,4},{4,8},{8,12},{12,16},{16,20},{20,24},{24,28},{1,5},{5,9},{9,... | collective-permute-start | bytes 1572872 | tf_op jit(solution)/shard_map/while/body/eval_jaxpr/ppermute | solution.py:15
  104.2 10.7 %collective-permute-start = (f32[8,128,128]{2,1,0:T(8,128)}, f32[8,128,128]{2,1,0:T(8,128)S(1)}, u32[]{:S(2)}, u32[]{:S(2)}) collective-permute-start(f32[8,128,128]{2,1,0:T(8,128)} %multiply_add_fusion.6), channel_id=1, source_target_pairs={{0,4},{4,8},{8,12},{12,16},{16,20},{20,24},{24,28},{1,5},{5,9},{9,... | collective-permute-start | bytes 1572872 | tf_op jit(solution)/shard_map/while/body/eval_jaxpr/ppermute | solution.py:15
  115.8 10.7 %collective-permute-start = (f32[8,128,128]{2,1,0:T(8,128)}, f32[8,128,128]{2,1,0:T(8,128)S(1)}, u32[]{:S(2)}, u32[]{:S(2)}) collective-permute-start(f32[8,128,128]{2,1,0:T(8,128)} %multiply_add_fusion.6), channel_id=1, source_target_pairs={{0,4},{4,8},{8,12},{12,16},{16,20},{20,24},{24,28},{1,5},{5,9},{9,... | collective-permute-start | bytes 1572872 | tf_op jit(solution)/shard_map/while/body/eval_jaxpr/ppermute | solution.py:15
  127.4 10.7 %collective-permute-start = (f32[8,128,128]{2,1,0:T(8,128)}, f32[8,128,128]{2,1,0:T(8,128)S(1)}, u32[]{:S(2)}, u32[]{:S(2)}) collective-permute-start(f32[8,128,128]{2,1,0:T(8,128)} %multiply_add_fusion.6), channel_id=1, source_target_pairs={{0,4},{4,8},{8,12},{12,16},{16,20},{20,24},{24,28},{1,5},{5,9},{9,... | collective-permute-start | bytes 1572872 | tf_op jit(solution)/shard_map/while/body/eval_jaxpr/ppermute | solution.py:15
  139.0 10.7 %collective-permute-start = (f32[8,128,128]{2,1,0:T(8,128)}, f32[8,128,128]{2,1,0:T(8,128)S(1)}, u32[]{:S(2)}, u32[]{:S(2)}) collective-permute-start(f32[8,128,128]{2,1,0:T(8,128)} %multiply_add_fusion.6), channel_id=1, source_target_pairs={{0,4},{4,8},{8,12},{12,16},{16,20},{20,24},{24,28},{1,5},{5,9},{9,... | collective-permute-start | bytes 1572872 | tf_op jit(solution)/shard_map/while/body/eval_jaxpr/ppermute | solution.py:15
  149.9 6.1 copy-start.55
  158.8 5.1 copy-start.60
  158.9 5.1 copy-start.16
  158.9 5.1 copy-start.25
  164.9 123.8 %copy-start.5 = (f32[128,1024]{1,0:T(8,128)}, f32[128,1024]{1,0:T(8,128)S(1)}, u32[]{:S(2)}) copy-start(f32[128,1024]{1,0:T(8,128)S(1)} %get-tuple-element.310) | copy-start | bytes 1572868
  164.9 123.8 %copy-start.68 = (f32[128]{0:T(128)}, f32[128]{0:T(128)S(1)}, u32[]{:S(2)}) copy-start(f32[128]{0:T(128)S(1)} %add_rsqrt_fusion.2) | copy-start | bytes 1540
  165.8 69.7 %all-gather.9.cloned.1.call-start = ((), (), s32[]{:S(2)}) async-start(), calls=%async_computation.5 | async-start | bytes 1310720 | tf_op jit(solution)/shard_map/all_gather | solution.py:161
  166.5 120.9 %reduce-scatter.5.cloned.1.call-start = ((), (), s32[]{:S(2)}) async-start(), calls=%async_computation.6 | async-start | bytes 2621440 | tf_op jit(solution)/shard_map/reduce_scatter | solution.py:168
  235.5 4.5 copy-start.83
  244.3 44.4 %copy-start.31 = (bf16[128,1024]{1,0:T(8,128)(2,1)S(1)}, bf16[128,1024]{1,0:T(8,128)(2,1)}, u32[]{:S(2)}) copy-start(bf16[128,1024]{1,0:T(8,128)(2,1)} %param.33) | copy-start | bytes 786436
  244.3 46.5 %copy-start.76 = (f32[1,8]{1,0:T(1,128)S(1)}, f32[1,8]{1,0:T(1,128)}, u32[]{:S(2)}) copy-start(f32[1,8]{1,0:T(1,128)} %get-tuple-element.303) | copy-start | bytes 100
  244.3 73.8 %all-gather.11.cloned.1.call-start = ((), (), s32[]{:S(2)}) async-start(), calls=%async_computation.7 | async-start | bytes 1310720 | tf_op jit(solution)/shard_map/all_gather | solution.py:176
  290.7 156.2 %reduce-scatter.3.cloned.1.call-start = ((), (), s32[]{:S(2)}) async-start(), calls=%async_computation.4 | async-start | bytes 1310720 | tf_op jit(solution)/shard_map/reduce_scatter | solution.py:157
  295.8 346.8 %all-reduce.4.cloned.1.call-start = ((), (), s32[]{:S(2)}) async-start(), calls=%async_computation.8 | async-start | bytes 29622272 | tf_op jit(solution)/shard_map/psum | solution.py:236
  301.7 16.3 %copy-start.61 = (f32[1,2,2,128]{3,1,2,0:T(2,128)S(1)}, f32[1,2,2,128]{3,1,2,0:T(2,128)}, u32[]{:S(2)}) copy-start(f32[1,2,2,128]{3,1,2,0:T(2,128)} %copy-done.60) | copy-start | bytes 6148
  318.1 6.1 copy-start.2
  325.0 5.0 copy-start.3
  339.2 67.9 %copy-start.67 = (f32[2,8]{1,0:T(2,128)S(1)}, f32[2,8]{1,0:T(2,128)}, u32[]{:S(2)}) copy-start(f32[2,8]{1,0:T(2,128)} %rev.8) | copy-start | bytes 196
  340.1 3.6 collective-permute-start.1
  346.4 6.9 %collective-permute-start.1 = (bf16[8,128,128]{2,1,0:T(8,128)(2,1)}, bf16[8,128,128]{2,1,0:T(8,128)(2,1)S(1)}, u32[]{:S(2)}, u32[]{:S(2)}) collective-permute-start(bf16[8,128,128]{2,1,0:T(8,128)(2,1)} %fusion.155), channel_id=1, source_target_pairs={{4,0},{8,4},{12,8},{16,12},{20,16},{24,20},{28,24},{5,1},{9,5},{13... | collective-permute-start | bytes 786440 | tf_op jit(solution)/shard_map/while/body/eval_jaxpr/ppermute | solution.py:15
  356.1 7.9 %collective-permute-start.1 = (bf16[8,128,128]{2,1,0:T(8,128)(2,1)}, bf16[8,128,128]{2,1,0:T(8,128)(2,1)S(1)}, u32[]{:S(2)}, u32[]{:S(2)}) collective-permute-start(bf16[8,128,128]{2,1,0:T(8,128)(2,1)} %fusion.155), channel_id=1, source_target_pairs={{4,0},{8,4},{12,8},{16,12},{20,16},{24,20},{28,24},{5,1},{9,5},{13... | collective-permute-start | bytes 786440 | tf_op jit(solution)/shard_map/while/body/eval_jaxpr/ppermute | solution.py:15
  366.7 7.9 %collective-permute-start.1 = (bf16[8,128,128]{2,1,0:T(8,128)(2,1)}, bf16[8,128,128]{2,1,0:T(8,128)(2,1)S(1)}, u32[]{:S(2)}, u32[]{:S(2)}) collective-permute-start(bf16[8,128,128]{2,1,0:T(8,128)(2,1)} %fusion.155), channel_id=1, source_target_pairs={{4,0},{8,4},{12,8},{16,12},{20,16},{24,20},{28,24},{5,1},{9,5},{13... | collective-permute-start | bytes 786440 | tf_op jit(solution)/shard_map/while/body/eval_jaxpr/ppermute | solution.py:15
  377.3 7.9 %collective-permute-start.1 = (bf16[8,128,128]{2,1,0:T(8,128)(2,1)}, bf16[8,128,128]{2,1,0:T(8,128)(2,1)S(1)}, u32[]{:S(2)}, u32[]{:S(2)}) collective-permute-start(bf16[8,128,128]{2,1,0:T(8,128)(2,1)} %fusion.155), channel_id=1, source_target_pairs={{4,0},{8,4},{12,8},{16,12},{20,16},{24,20},{28,24},{5,1},{9,5},{13... | collective-permute-start | bytes 786440 | tf_op jit(solution)/shard_map/while/body/eval_jaxpr/ppermute | solution.py:15
  387.9 7.9 %collective-permute-start.1 = (bf16[8,128,128]{2,1,0:T(8,128)(2,1)}, bf16[8,128,128]{2,1,0:T(8,128)(2,1)S(1)}, u32[]{:S(2)}, u32[]{:S(2)}) collective-permute-start(bf16[8,128,128]{2,1,0:T(8,128)(2,1)} %fusion.155), channel_id=1, source_target_pairs={{4,0},{8,4},{12,8},{16,12},{20,16},{24,20},{28,24},{5,1},{9,5},{13... | collective-permute-start | bytes 786440 | tf_op jit(solution)/shard_map/while/body/eval_jaxpr/ppermute | solution.py:15
  398.4 7.9 %collective-permute-start.1 = (bf16[8,128,128]{2,1,0:T(8,128)(2,1)}, bf16[8,128,128]{2,1,0:T(8,128)(2,1)S(1)}, u32[]{:S(2)}, u32[]{:S(2)}) collective-permute-start(bf16[8,128,128]{2,1,0:T(8,128)(2,1)} %fusion.155), channel_id=1, source_target_pairs={{4,0},{8,4},{12,8},{16,12},{20,16},{24,20},{28,24},{5,1},{9,5},{13... | collective-permute-start | bytes 786440 | tf_op jit(solution)/shard_map/while/body/eval_jaxpr/ppermute | solution.py:15
  407.2 4.1 copy-start.4
  407.2 4.1 copy-start.20
  412.9 18.4 %copy-start.51 = (bf16[2,256,8,128]{3,2,1,0:T(8,128)(2,1)}, bf16[2,256,8,128]{3,2,1,0:T(8,128)(2,1)S(1)}, u32[]{:S(2)}) copy-start(bf16[2,256,8,128]{3,2,1,0:T(8,128)(2,1)S(1)} %copy.126) | copy-start | bytes 3145732
  642.5 4.2 copy-start.35
  (61 other events, 128.6 us)
Sparse Core Ops, SparseCore 0:
  9.6 30.6 all-gather.4
  165.9 40.6 all-gather.6
  208.1 27.3 all-gather.8
  244.4 42.9 reduce-scatter.4
  290.8 27.2 all-gather.10
  320.2 26.6 reduce-scatter.2
  436.9 205.6 all-reduce.3
where the time goes:
time: 678 us; the launch traced here: 670 us
  waiting for transfers between devices  395 us (58%)
  matrix products  95.5 us (14%)
  other arithmetic  66.9 us (10%)
  starting transfers between devices  64.5 us (10%)
  local copies, waits for them, and re-layouts  30.2 us (4%)
  between operations  16.5 us (2%)
    psum x1, waiting for transfers between devices, body(): lax.psum(weight_grad(normed_one, grad_query_lin).astype(jnp.bfloat16), 'w...  193 us
    ppermute x14, starting transfers between devices, from_behind(): return lax.ppermute(block, axis, route)  64 us
    ppermute x14, waiting for transfers between devices, from_behind(): return lax.ppermute(block, axis, route)  52.8 us
    reduce_scatter x1, waiting for transfers between devices, body(): lax.psum_scatter(transposed(grad_first, w_first) + transposed(grad_second...  43.1 us
    all_gather x1, waiting for transfers between devices, body(): gathered_two = lax.all_gather(normed_two, 'narrow', axis=0, tiled=True)  40 us
    all_gather x1, waiting for transfers between devices, body(): whole_rows = lax.all_gather(tokens, 'narrow', axis=0, tiled=True)  27.8 us
    all_gather x1, waiting for transfers between devices, body(): grad_whole = lax.all_gather(cotangent, 'narrow', axis=0, tiled=True)  23 us
    dot_general x8, matrix products, project(): return jnp.dot(left_hand, right_hand, preferred_element_type=jnp.float32)  22.8 us
  transfers between devices with their start and end apart: 21, of which 20 were waited for; matrix products, arithmetic and copies ran while one was open for 14% of the time, Pallas kernels for 0%

commit v1 on v0

--- a/solution.py
+++ b/solution.py
@@ -233,9 +233,10 @@
     grad_own = lax.dynamic_slice_in_dim(grad_normed_one, own_start, share_rows, 0)
     grad_tokens = grad_hidden + rms_back(tokens.astype(jnp.float32), grad_own)
     summed = (
-        lax.psum(weight_grad(normed_one, grad_query_lin).astype(jnp.bfloat16), "wide").astype(
-            jnp.float32
-        ),
+        jnp.sum(
+            lax.all_gather(weight_grad(normed_one, grad_query_lin).astype(jnp.bfloat16), "wide"),
+            axis=0,
+        ).astype(jnp.float32),
         lax.psum(weight_grad(normed_one, grad_key_lin).astype(jnp.bfloat16), "wide").astype(
             jnp.float32
         ),

time: 678 us -> 735 us (1.084)
  waiting for transfers between devices: 395 us -> 436 us
  other arithmetic: 66.9 us -> 79.6 us
    all_gather x0 -> x1, waiting for transfers between devices: none -> 74.7 us  [body(): lax.all_gather(weight_grad(normed_one, grad_query_lin).astype(jnp.bfloat1...]
    psum x1, waiting for transfers between devices: 193 us -> 159 us  [body(): lax.psum(weight_grad(normed_one, grad_key_lin).astype(jnp.bfloat16), 'wide')]
    reduce_sum x0 -> x1, other arithmetic: none -> 10.8 us  [body(): jnp.sum(lax.all_gather(weight_grad(normed_one, grad_query_lin).astype(jnp...]
    unnamed x181 -> x179, local copies, waits for them, and re-layouts: 12.8 us -> 15.1 us
  transfers between devices with their start and end apart: 21 -> 22, of which waited for: 20 -> 21; matrix products, arithmetic and copies ran while one was open for 14% -> 16% of each run, Pallas kernels for 0% -> 0%
where the time goes in v1:
time: 735 us; the launch traced here: 726 us
  waiting for transfers between devices  436 us (59%)
  matrix products  96 us (13%)
  other arithmetic  79.6 us (11%)
  starting transfers between devices  64.7 us (9%)
  local copies, waits for them, and re-layouts  32.6 us (4%)
  between operations  16.5 us (2%)
    psum x1, waiting for transfers between devices, body(): lax.psum(weight_grad(normed_one, grad_key_lin).astype(jnp.bfloat16), 'wide')  159 us
    all_gather x1, waiting for transfers between devices, body(): lax.all_gather(weight_grad(normed_one, grad_query_lin).astype(jnp.bfloat1...  74.7 us
    ppermute x14, starting transfers between devices, from_behind(): return lax.ppermute(block, axis, route)  64 us
    ppermute x14, waiting for transfers between devices, from_behind(): return lax.ppermute(block, axis, route)  53 us
    reduce_scatter x1, waiting for transfers between devices, body(): lax.psum_scatter(transposed(grad_first, w_first) + transposed(grad_second...  43.1 us
    all_gather x1, waiting for transfers between devices, body(): gathered_two = lax.all_gather(normed_two, 'narrow', axis=0, tiled=True)  40 us
    all_gather x1, waiting for transfers between devices, body(): whole_rows = lax.all_gather(tokens, 'narrow', axis=0, tiled=True)  27.8 us
    all_gather x1, waiting for transfers between devices, body(): grad_whole = lax.all_gather(cotangent, 'narrow', axis=0, tiled=True)  23 us
  transfers between devices with their start and end apart: 22, of which 21 were waited for; matrix products, arithmetic and copies ran while one was open for 16% of the time, Pallas kernels for 0%

profile of v1, /device:TPU:0, one launch (start us, length us, event | category | flops | bytes accessed | tf_op | source)
XLA Modules:
  0.0 725.9 jit_solution(15662212976881553449)
XLA Ops:
  12.5 27.8 %all-gather.7.cloned.1.call-done = bf16[512,1024]{1,0:T(8,128)(2,1)} async-done(((bf16[128,1024]{1,0:T(8,128)(2,1)}), bf16[512,1024]{1,0:T(8,128)(2,1)}) %all-gather.7.cloned.1.call-update) | async-done | bytes 1048592 | tf_op jit(solution)/shard_map/all_gather | solution.py:94
  41.8 3.2 fusion.96
  50.8 3.2 fusion.94
  60.0 3.5 fusion.12
  64.6 4.1 while.52
  71.1 3.1 multiply_convert_fusion.1
  76.4 73.5 %while.51 = (s32[]{:T(128)}, f32[8,128,128]{2,1,0:T(8,128)S(1)}, f32[8]{0:T(128)S(1)}, f32[8,128,128]{2,1,0:T(8,128)S(1)}, s32[]{:T(128)}) while((s32[]{:T(128)}, f32[8,128,128]{2,1,0:T(8,128)S(1)}, f32[8]{0:T(128)S(1)}, f32[8,128,128]{2,1,0:T(8,128)S(1)}, s32[]{:T(128)}) %tuple.105), condition=%wide.region_8.9_spmd, body=%wide.region_7.8_spmd.sunk | while | flops 262146 | bytes 3670149 | solution.py:137
  81.3 8.8 %collective-permute-start = (f32[8,128,128]{2,1,0:T(8,128)}, f32[8,128,128]{2,1,0:T(8,128)S(1)}, u32[]{:S(2)}, u32[]{:S(2)}) collective-permute-start(f32[8,128,128]{2,1,0:T(8,128)} %multiply_add_fusion.6), channel_id=1, source_target_pairs={{0,4},{4,8},{8,12},{12,16},{16,20},{20,24},{24,28},{1,5},{5,9},{9,... | collective-permute-start | bytes 1572872 | tf_op jit(solution)/shard_map/while/body/eval_jaxpr/ppermute | solution.py:15
  92.7 9.0 %collective-permute-start = (f32[8,128,128]{2,1,0:T(8,128)}, f32[8,128,128]{2,1,0:T(8,128)S(1)}, u32[]{:S(2)}, u32[]{:S(2)}) collective-permute-start(f32[8,128,128]{2,1,0:T(8,128)} %multiply_add_fusion.6), channel_id=1, source_target_pairs={{0,4},{4,8},{8,12},{12,16},{16,20},{20,24},{24,28},{1,5},{5,9},{9,... | collective-permute-start | bytes 1572872 | tf_op jit(solution)/shard_map/while/body/eval_jaxpr/ppermute | solution.py:15
  104.3 9.0 %collective-permute-start = (f32[8,128,128]{2,1,0:T(8,128)}, f32[8,128,128]{2,1,0:T(8,128)S(1)}, u32[]{:S(2)}, u32[]{:S(2)}) collective-permute-start(f32[8,128,128]{2,1,0:T(8,128)} %multiply_add_fusion.6), channel_id=1, source_target_pairs={{0,4},{4,8},{8,12},{12,16},{16,20},{20,24},{24,28},{1,5},{5,9},{9,... | collective-permute-start | bytes 1572872 | tf_op jit(solution)/shard_map/while/body/eval_jaxpr/ppermute | solution.py:15
  115.9 9.0 %collective-permute-start = (f32[8,128,128]{2,1,0:T(8,128)}, f32[8,128,128]{2,1,0:T(8,128)S(1)}, u32[]{:S(2)}, u32[]{:S(2)}) collective-permute-start(f32[8,128,128]{2,1,0:T(8,128)} %multiply_add_fusion.6), channel_id=1, source_target_pairs={{0,4},{4,8},{8,12},{12,16},{16,20},{20,24},{24,28},{1,5},{5,9},{9,... | collective-permute-start | bytes 1572872 | tf_op jit(solution)/shard_map/while/body/eval_jaxpr/ppermute | solution.py:15
  127.5 9.0 %collective-permute-start = (f32[8,128,128]{2,1,0:T(8,128)}, f32[8,128,128]{2,1,0:T(8,128)S(1)}, u32[]{:S(2)}, u32[]{:S(2)}) collective-permute-start(f32[8,128,128]{2,1,0:T(8,128)} %multiply_add_fusion.6), channel_id=1, source_target_pairs={{0,4},{4,8},{8,12},{12,16},{16,20},{20,24},{24,28},{1,5},{5,9},{9,... | collective-permute-start | bytes 1572872 | tf_op jit(solution)/shard_map/while/body/eval_jaxpr/ppermute | solution.py:15
  139.1 9.0 %collective-permute-start = (f32[8,128,128]{2,1,0:T(8,128)}, f32[8,128,128]{2,1,0:T(8,128)S(1)}, u32[]{:S(2)}, u32[]{:S(2)}) collective-permute-start(f32[8,128,128]{2,1,0:T(8,128)} %multiply_add_fusion.6), channel_id=1, source_target_pairs={{0,4},{4,8},{8,12},{12,16},{16,20},{20,24},{24,28},{1,5},{5,9},{9,... | collective-permute-start | bytes 1572872 | tf_op jit(solution)/shard_map/while/body/eval_jaxpr/ppermute | solution.py:15
  150.0 6.0 multiply_reduce_fusion.1
  156.0 2.9 copy.119
  159.0 5.0 multiply_convert_fusion.4
  166.7 40.0 %all-gather.9.cloned.1.call-done = bf16[512,1024]{1,0:T(8,128)(2,1)} async-done(((bf16[128,1024]{1,0:T(8,128)(2,1)}), bf16[512,1024]{1,0:T(8,128)(2,1)}) %all-gather.9.cloned.1.call-update) | async-done | bytes 1048592 | tf_op jit(solution)/shard_map/all_gather | solution.py:153
  206.7 3.9 fusion.100
  212.6 23.0 %all-gather.11.cloned.1.call-done = bf16[512,1024]{1,0:T(8,128)(2,1)} async-done(((bf16[128,1024]{1,0:T(8,128)(2,1)}), bf16[512,1024]{1,0:T(8,128)(2,1)}) %all-gather.11.cloned.1.call-update) | async-done | bytes 1048592 | tf_op jit(solution)/shard_map/all_gather | solution.py:161
  235.6 4.5 multiply_convert_fusion.7
  244.5 43.1 %reduce-scatter.5.cloned.1.call-done = f32[128,1024]{1,0:T(8,128)} async-done(((f32[512,1024]{1,0:T(8,128)}), f32[128,1024]{1,0:T(8,128)}) %reduce-scatter.5.cloned.1.call-update) | async-done | bytes 524304 | tf_op jit(solution)/shard_map/reduce_scatter | solution.py:168
  292.4 3.6 convolution_convert_fusion.8
  296.2 3.7 convolution_convert_fusion.6
  304.0 14.1 %all-gather.13.cloned.1.call-done = bf16[512,1024]{1,0:T(8,128)(2,1)} async-done(((bf16[128,1024]{1,0:T(8,128)(2,1)}), bf16[512,1024]{1,0:T(8,128)(2,1)}) %all-gather.13.cloned.1.call-update) | async-done | bytes 1048592 | tf_op jit(solution)/shard_map/all_gather | solution.py:176
  318.2 6.1 multiply_reduce_fusion
  328.7 2.6 multiply_convert_fusion
  332.4 4.0 while.53
  336.4 68.0 %while.54 = (s32[]{:T(128)}, f32[8,128,128]{2,1,0:T(8,128)}, f32[8]{0:T(128)S(1)}, f32[8,128,128]{2,1,0:T(8,128)S(1)}, s32[]{:T(128)}, /*index=5*/s32[]{:T(128)}) while((s32[]{:T(128)}, f32[8,128,128]{2,1,0:T(8,128)}, f32[8]{0:T(128)S(1)}, f32[8,128,128]{2,1,0:T(8,128)S(1)}, s32[]{:T(128)}, /*index=5*/s32[]{:T(128)}) %tuple.131), condition=%wide.region_20.21_spmd.clone, body=%wide.region_19.20_spmd.clone.sunk | while | flops 655363 | bytes 3145879 | solution.py:214
  344.9 5.8 collective-permute-done.1
  354.6 6.6 collective-permute-done.1
  365.2 6.6 collective-permute-done.1
  375.8 6.6 collective-permute-done.1
  386.4 6.6 collective-permute-done.1
  397.0 6.6 collective-permute-done.1
  404.5 4.1 fusion.11
  416.8 2.6 convolution_convert_fusion
  420.6 2.7 convolution_convert_fusion.3
  423.4 2.7 convolution_convert_fusion.2
  426.1 2.7 convolution_convert_fusion.1
  429.1 2.7 fusion.32
  436.8 2.7 convolution_convert_fusion.4
  440.6 2.7 fusion.106
  452.7 159.0 %all-reduce.4.cloned.1.call-done = (bf16[1024,1024]{1,0:T(8,128)(2,1)}, bf16[1024,1024]{1,0:T(8,128)(2,1)}, bf16[1024,1024]{1,0:T(8,128)(2,1)}, bf16[1024,1024]{...) async-done(((bf16[1024,1024]{1,0:T(8,128)(2,1)}, bf16[1024,1024]{1,0:T(8,128)(2,1)}, ...) | async-done | bytes 12714000 | tf_op jit(solution)/shard_map/psum | solution.py:240
  611.7 4.2 convert_element_type.180
  620.9 2.7 convert_element_type.186
  629.4 74.7 %all-gather.15.cloned.1.call-done = bf16[8192,1024]{1,0:T(8,128)(2,1)} async-done(((bf16[1024,1024]{1,0:T(8,128)(2,1)}), bf16[8192,1024]{1,0:T(8,128)(2,1)}) %all-gather.15.cloned.1.call-update) | async-done | bytes 16777232 | tf_op jit(solution)/shard_map/all_gather | solution.py:237
  704.1 10.8 %reduce_sum.94 = bf16[1024,1024]{1,0:T(8,128)(2,1)} reduce(bf16[8,1024,1024]{2,1,0:T(8,128)(2,1)} %bitcast.227, bf16[]{:T(256)} %constant.110.clone.1), dimensions={0}, to_apply=%region_22.23 | reduce | flops 7340032 | bytes 18874370 | tf_op jit(solution)/shard_map/reduce_sum | solution.py:236
  714.9 4.1 convert_element_type.178
  (319 shorter events, 139.0 us)
Async XLA Ops:
  7.2 151.8 %copy-start = (bf16[1024,1024]{1,0:T(8,128)(2,1)S(1)}, bf16[1024,1024]{1,0:T(8,128)(2,1)}, u32[]{:S(2)}) copy-start(bf16[1024,1024]{1,0:T(8,128)(2,1)} %param.28) | copy-start | bytes 6291460
  7.2 33.1 %all-gather.7.cloned.1.call-start = ((), (), s32[]{:S(2)}) async-start(), calls=%async_computation.2 | async-start | bytes 1310720 | tf_op jit(solution)/shard_map/all_gather | solution.py:94
  7.9 198.7 %all-gather.9.cloned.1.call-start = ((), (), s32[]{:S(2)}) async-start(), calls=%async_computation.3 | async-start | bytes 1310720 | tf_op jit(solution)/shard_map/all_gather | solution.py:153
  10.1 35.0 %copy-start.58 = (f32[8,2,2]{0,1,2:T(2,128)}, f32[8,2,2]{0,1,2:T(2,128)S(1)}, u32[]{:S(2)}) copy-start(f32[8,2,2]{0,1,2:T(2,128)S(1)} %copy.112) | copy-start | bytes 388
  11.5 138.5 %copy-start.69 = (f32[2]{0:T(128)}, f32[2]{0:T(128)S(1)}, u32[]{:S(2)}) copy-start(f32[2]{0:T(128)S(1)} %fusion.84) | copy-start | bytes 28
  11.6 59.5 %copy-start.56 = (f32[2,8,256]{2,1,0:T(8,128)}, f32[2,8,256]{2,1,0:T(8,128)S(1)}, u32[]{:S(2)}) copy-start(f32[2,8,256]{2,1,0:T(8,128)S(1)} %bitcast_bitcast_fusion.1) | copy-start | bytes 49156
  11.7 33.3 %copy-start.63 = (f32[2,8]{1,0:T(2,128)}, f32[2,8]{1,0:T(2,128)S(1)}, u32[]{:S(2)}) copy-start(f32[2,8]{1,0:T(2,128)S(1)} %slice_reduce_fusion) | copy-start | bytes 196
  12.4 137.6 %copy-start.64 = (f32[2,8]{1,0:T(2,128)}, f32[2,8]{1,0:T(2,128)S(1)}, u32[]{:S(2)}) copy-start(f32[2,8]{1,0:T(2,128)S(1)} %reduce_window.14) | copy-start | bytes 196
  12.4 41.6 %copy-start.61 = (f32[512]{0:T(512)}, f32[512]{0:T(512)S(1)}, u32[]{:S(2)}) copy-start(f32[512]{0:T(512)S(1)} %fusion.81) | copy-start | bytes 6148
  41.8 117.1 %copy-start.73 = (f32[512]{0:T(512)}, f32[512]{0:T(512)S(1)}, u32[]{:S(2)}) copy-start(f32[512]{0:T(512)S(1)} %add_rsqrt_fusion) | copy-start | bytes 6148
  58.9 4.6 copy-start.10
  68.7 5.5 copy-start.71
  77.3 3.0 collective-permute-start
  81.3 10.5 %collective-permute-start = (f32[8,128,128]{2,1,0:T(8,128)}, f32[8,128,128]{2,1,0:T(8,128)S(1)}, u32[]{:S(2)}, u32[]{:S(2)}) collective-permute-start(f32[8,128,128]{2,1,0:T(8,128)} %multiply_add_fusion.6), channel_id=1, source_target_pairs={{0,4},{4,8},{8,12},{12,16},{16,20},{20,24},{24,28},{1,5},{5,9},{9,... | collective-permute-start | bytes 1572872 | tf_op jit(solution)/shard_map/while/body/eval_jaxpr/ppermute | solution.py:15
  92.7 10.7 %collective-permute-start = (f32[8,128,128]{2,1,0:T(8,128)}, f32[8,128,128]{2,1,0:T(8,128)S(1)}, u32[]{:S(2)}, u32[]{:S(2)}) collective-permute-start(f32[8,128,128]{2,1,0:T(8,128)} %multiply_add_fusion.6), channel_id=1, source_target_pairs={{0,4},{4,8},{8,12},{12,16},{16,20},{20,24},{24,28},{1,5},{5,9},{9,... | collective-permute-start | bytes 1572872 | tf_op jit(solution)/shard_map/while/body/eval_jaxpr/ppermute | solution.py:15
  104.3 10.7 %collective-permute-start = (f32[8,128,128]{2,1,0:T(8,128)}, f32[8,128,128]{2,1,0:T(8,128)S(1)}, u32[]{:S(2)}, u32[]{:S(2)}) collective-permute-start(f32[8,128,128]{2,1,0:T(8,128)} %multiply_add_fusion.6), channel_id=1, source_target_pairs={{0,4},{4,8},{8,12},{12,16},{16,20},{20,24},{24,28},{1,5},{5,9},{9,... | collective-permute-start | bytes 1572872 | tf_op jit(solution)/shard_map/while/body/eval_jaxpr/ppermute | solution.py:15
  115.9 10.7 %collective-permute-start = (f32[8,128,128]{2,1,0:T(8,128)}, f32[8,128,128]{2,1,0:T(8,128)S(1)}, u32[]{:S(2)}, u32[]{:S(2)}) collective-permute-start(f32[8,128,128]{2,1,0:T(8,128)} %multiply_add_fusion.6), channel_id=1, source_target_pairs={{0,4},{4,8},{8,12},{12,16},{16,20},{20,24},{24,28},{1,5},{5,9},{9,... | collective-permute-start | bytes 1572872 | tf_op jit(solution)/shard_map/while/body/eval_jaxpr/ppermute | solution.py:15
  127.5 10.7 %collective-permute-start = (f32[8,128,128]{2,1,0:T(8,128)}, f32[8,128,128]{2,1,0:T(8,128)S(1)}, u32[]{:S(2)}, u32[]{:S(2)}) collective-permute-start(f32[8,128,128]{2,1,0:T(8,128)} %multiply_add_fusion.6), channel_id=1, source_target_pairs={{0,4},{4,8},{8,12},{12,16},{16,20},{20,24},{24,28},{1,5},{5,9},{9,... | collective-permute-start | bytes 1572872 | tf_op jit(solution)/shard_map/while/body/eval_jaxpr/ppermute | solution.py:15
  139.1 10.7 %collective-permute-start = (f32[8,128,128]{2,1,0:T(8,128)}, f32[8,128,128]{2,1,0:T(8,128)S(1)}, u32[]{:S(2)}, u32[]{:S(2)}) collective-permute-start(f32[8,128,128]{2,1,0:T(8,128)} %multiply_add_fusion.6), channel_id=1, source_target_pairs={{0,4},{4,8},{8,12},{12,16},{16,20},{20,24},{24,28},{1,5},{5,9},{9,... | collective-permute-start | bytes 1572872 | tf_op jit(solution)/shard_map/while/body/eval_jaxpr/ppermute | solution.py:15
  150.0 6.0 copy-start.54
  158.9 5.1 copy-start.59
  158.9 5.1 copy-start.16
  159.0 5.1 copy-start.24
  165.0 123.8 %copy-start.6 = (f32[128,1024]{1,0:T(8,128)}, f32[128,1024]{1,0:T(8,128)S(1)}, u32[]{:S(2)}) copy-start(f32[128,1024]{1,0:T(8,128)S(1)} %get-tuple-element.309) | copy-start | bytes 1572868
  165.0 123.8 %copy-start.67 = (f32[128]{0:T(128)}, f32[128]{0:T(128)S(1)}, u32[]{:S(2)}) copy-start(f32[128]{0:T(128)S(1)} %add_rsqrt_fusion.2) | copy-start | bytes 1540
  165.9 69.7 %all-gather.11.cloned.1.call-start = ((), (), s32[]{:S(2)}) async-start(), calls=%async_computation.5 | async-start | bytes 1310720 | tf_op jit(solution)/shard_map/all_gather | solution.py:161
  166.6 120.9 %reduce-scatter.5.cloned.1.call-start = ((), (), s32[]{:S(2)}) async-start(), calls=%async_computation.6 | async-start | bytes 2621440 | tf_op jit(solution)/shard_map/reduce_scatter | solution.py:168
  235.6 4.5 copy-start.82
  244.4 44.4 %copy-start.30 = (bf16[128,1024]{1,0:T(8,128)(2,1)S(1)}, bf16[128,1024]{1,0:T(8,128)(2,1)}, u32[]{:S(2)}) copy-start(bf16[128,1024]{1,0:T(8,128)(2,1)} %param.33) | copy-start | bytes 786436
  244.4 46.5 %copy-start.75 = (f32[1,8]{1,0:T(1,128)S(1)}, f32[1,8]{1,0:T(1,128)}, u32[]{:S(2)}) copy-start(f32[1,8]{1,0:T(1,128)} %get-tuple-element.302) | copy-start | bytes 100
  244.4 73.7 %all-gather.13.cloned.1.call-start = ((), (), s32[]{:S(2)}) async-start(), calls=%async_computation.7 | async-start | bytes 1310720 | tf_op jit(solution)/shard_map/all_gather | solution.py:176
  290.8 159.2 %reduce-scatter.3.cloned.1.call-start = ((), (), s32[]{:S(2)}) async-start(), calls=%async_computation.4 | async-start | bytes 1310720 | tf_op jit(solution)/shard_map/reduce_scatter | solution.py:157
  296.0 315.7 %all-reduce.4.cloned.1.call-start = ((), (), s32[]{:S(2)}) async-start(), calls=%async_computation.9 | async-start | bytes 25427968 | tf_op jit(solution)/shard_map/psum | solution.py:240
  302.0 16.2 %copy-start.60 = (f32[1,2,2,128]{3,1,2,0:T(2,128)S(1)}, f32[1,2,2,128]{3,1,2,0:T(2,128)}, u32[]{:S(2)}) copy-start(f32[1,2,2,128]{3,1,2,0:T(2,128)} %copy-done.59) | copy-start | bytes 6148
  318.2 6.1 copy-start.2
  325.1 6.2 copy-start.3
  336.4 68.0 %copy-start.66 = (f32[2,8]{1,0:T(2,128)S(1)}, f32[2,8]{1,0:T(2,128)}, u32[]{:S(2)}) copy-start(f32[2,8]{1,0:T(2,128)} %rev.8) | copy-start | bytes 196
  337.3 3.6 collective-permute-start.1
  343.6 7.0 collective-permute-start.1
  353.4 7.9 %collective-permute-start.1 = (bf16[8,128,128]{2,1,0:T(8,128)(2,1)}, bf16[8,128,128]{2,1,0:T(8,128)(2,1)S(1)}, u32[]{:S(2)}, u32[]{:S(2)}) collective-permute-start(bf16[8,128,128]{2,1,0:T(8,128)(2,1)} %fusion.155), channel_id=1, source_target_pairs={{4,0},{8,4},{12,8},{16,12},{20,16},{24,20},{28,24},{5,1},{9,5},{13... | collective-permute-start | bytes 786440 | tf_op jit(solution)/shard_map/while/body/eval_jaxpr/ppermute | solution.py:15
  363.9 7.9 %collective-permute-start.1 = (bf16[8,128,128]{2,1,0:T(8,128)(2,1)}, bf16[8,128,128]{2,1,0:T(8,128)(2,1)S(1)}, u32[]{:S(2)}, u32[]{:S(2)}) collective-permute-start(bf16[8,128,128]{2,1,0:T(8,128)(2,1)} %fusion.155), channel_id=1, source_target_pairs={{4,0},{8,4},{12,8},{16,12},{20,16},{24,20},{28,24},{5,1},{9,5},{13... | collective-permute-start | bytes 786440 | tf_op jit(solution)/shard_map/while/body/eval_jaxpr/ppermute | solution.py:15
  374.5 7.9 %collective-permute-start.1 = (bf16[8,128,128]{2,1,0:T(8,128)(2,1)}, bf16[8,128,128]{2,1,0:T(8,128)(2,1)S(1)}, u32[]{:S(2)}, u32[]{:S(2)}) collective-permute-start(bf16[8,128,128]{2,1,0:T(8,128)(2,1)} %fusion.155), channel_id=1, source_target_pairs={{4,0},{8,4},{12,8},{16,12},{20,16},{24,20},{28,24},{5,1},{9,5},{13... | collective-permute-start | bytes 786440 | tf_op jit(solution)/shard_map/while/body/eval_jaxpr/ppermute | solution.py:15
  385.1 7.9 %collective-permute-start.1 = (bf16[8,128,128]{2,1,0:T(8,128)(2,1)}, bf16[8,128,128]{2,1,0:T(8,128)(2,1)S(1)}, u32[]{:S(2)}, u32[]{:S(2)}) collective-permute-start(bf16[8,128,128]{2,1,0:T(8,128)(2,1)} %fusion.155), channel_id=1, source_target_pairs={{4,0},{8,4},{12,8},{16,12},{20,16},{24,20},{28,24},{5,1},{9,5},{13... | collective-permute-start | bytes 786440 | tf_op jit(solution)/shard_map/while/body/eval_jaxpr/ppermute | solution.py:15
  395.7 7.9 %collective-permute-start.1 = (bf16[8,128,128]{2,1,0:T(8,128)(2,1)}, bf16[8,128,128]{2,1,0:T(8,128)(2,1)S(1)}, u32[]{:S(2)}, u32[]{:S(2)}) collective-permute-start(bf16[8,128,128]{2,1,0:T(8,128)(2,1)} %fusion.155), channel_id=1, source_target_pairs={{4,0},{8,4},{12,8},{16,12},{20,16},{24,20},{28,24},{5,1},{9,5},{13... | collective-permute-start | bytes 786440 | tf_op jit(solution)/shard_map/while/body/eval_jaxpr/ppermute | solution.py:15
  404.5 4.1 copy-start.20
  411.1 12.3 %copy-start.50 = (bf16[2,256,8,128]{3,2,1,0:T(8,128)(2,1)}, bf16[2,256,8,128]{3,2,1,0:T(8,128)(2,1)S(1)}, u32[]{:S(2)}) copy-start(bf16[2,256,8,128]{3,2,1,0:T(8,128)(2,1)S(1)} %copy.126) | copy-start | bytes 3145732
  428.8 275.3 %all-gather.15.cloned.1.call-start = ((), (), s32[]{:S(2)}) async-start(), calls=%async_computation.8 | async-start | bytes 18874368 | tf_op jit(solution)/shard_map/all_gather | solution.py:237
  611.7 4.2 copy-start.33
  (61 other events, 130.8 us)
Sparse Core Ops, SparseCore 0:
  9.6 30.6 all-gather.6
  166.0 40.5 all-gather.8
  208.2 27.3 all-gather.10
  244.6 42.9 reduce-scatter.4
  290.9 27.1 all-gather.12
  320.3 26.6 reduce-scatter.2
  428.9 182.7 all-reduce.3
  614.1 89.8 all-gather.14
